TPU v7x, 128 devices: a whole 4x4x4 slice. The times are simulated.
128 devices in a mesh: subset: 8 (over y, z_lo), tile: 16 (over z_hi, x, core).
Axes of the slice: x: 4, y: 4, z: 4 (z_hi: 2, z_lo: 2; z = z_hi * 2 + z_lo), core: 2. Of those that a mesh axis runs over, the one named last changes fastest.
Arguments:
- start_volume: bfloat16 [8, 64, 65536], P(None, None, 'tile'), may hold values from 0 to 2
- measured: bfloat16 [8, 8, 64, 2048], P('subset'), may hold values from 6528 to 26112
- system_values: bfloat16 [8, 2048, 65536], P('subset', None, 'tile'), may hold values from 0.05 to 2088.96, as said below
- block_pattern: int32 [8, 16, 512], P('subset', None, 'tile'), may hold values from 0 to 1, as said below
- subset_order: int32 [64, 8], replicated, may hold values from 0 to 7, each once within a row
Outputs:
- volume_out: bfloat16 [8, 64, 65536], P(None, None, 'tile')
Inputs may be any that keep to these rules, and one draw needn't show every extreme that they name: `block_pattern`: each entry is 0 or 1; every block row and every block column of each subset's matrix within every 4096-voxel tile holds at least one 1. `system_values`: positive entries. `subset_order`: each row is a permutation of the 8 subsets.
All inputs are finite; a program needn't handle non-finite values.
Results may differ from a plain program's by a relative error of at most 0.0034.
Values may be sent and summed in bfloat16 or wider, within the bound.
A program may use at most 128 MiB of HBM per device.

v0:
```python
import jax
import jax.numpy as jnp
from jax import lax
from jax.sharding import PartitionSpec as P

BLOCK_SIDE = 128
SWEEP_PASSES = 4


def passed_along(block, axis, distance):
    devices = range(lax.axis_size(axis))
    route = [((i - distance) % len(devices), i) for i in devices]
    return lax.ppermute(block, axis, route)


def body(start_volume, measured, system_values, block_pattern, subset_order):
    owner_idx = lax.axis_index("subset")
    holder_count = lax.axis_size("subset")
    pattern = block_pattern[0].astype(jnp.bfloat16)
    matrix = system_values[0] * jnp.repeat(jnp.repeat(pattern, BLOCK_SIDE, 0), BLOCK_SIDE, 1)
    column_sum = jnp.sum(matrix, axis=0, dtype=jnp.float32)
    row_part = jnp.sum(matrix, axis=1, dtype=jnp.float32)[None, :]
    slice_measurement = measured[0]

    def subset_selector(slice_portion):
        source = (owner_idx - slice_portion) % holder_count
        return (subset_order == source).astype(jnp.bfloat16)

    volume = jnp.einsum(
        "sf,fsv->sv", subset_selector(0), start_volume, preferred_element_type=jnp.float32
    )
    ray_total = lax.psum(row_part, "tile")
    for slice_portion in range(SWEEP_PASSES):
        selected_subset = subset_selector(slice_portion)
        destination_rows = jnp.einsum(
            "ej,jev->ev", selected_subset, slice_measurement, preferred_element_type=jnp.float32
        )
        narrow = volume.astype(jnp.bfloat16)
        partial_value = lax.dot_general(
            narrow, matrix, (((1,), (1,)), ((), ())), preferred_element_type=jnp.float32
        )
        projected = lax.psum(partial_value, "tile")
        residue = ((destination_rows - projected) / ray_total).astype(jnp.bfloat16)
        spread_back = jnp.dot(residue, matrix, preferred_element_type=jnp.float32)
        volume = volume + spread_back / column_sum[None, :]
        if slice_portion + 1 < SWEEP_PASSES:
            volume = passed_along(volume, "subset", 1)
    final_pick = subset_selector(SWEEP_PASSES - 1).astype(jnp.float32)
    rounded = lax.optimization_barrier(volume.astype(jnp.bfloat16)).astype(jnp.float32)
    contribution = jnp.transpose(final_pick)[:, :, None] * rounded[None, :, :]
    gathered = lax.psum(contribution.astype(jnp.bfloat16), "subset")
    return gathered


def solution(mesh):
    placed = (
        P(None, None, "tile"),
        P("subset", None, None, None),
        P("subset", None, "tile"),
        P("subset", None, "tile"),
        P(),
    )
    return jax.shard_map(
        body, mesh=mesh, in_specs=placed, out_specs=P(None, None, "tile"), check_vma=False
    )
```

profile of v0, /device:TPU:16, one launch (start us, length us, event | category | flops | bytes accessed | tf_op | source)
XLA Modules:
  0.0 966.0 jit_solution(6587851373304264414)
XLA Ops:
  6.5 0.8 convert_bitcast_fusion.1
  7.4 0.7 convert_bitcast_fusion
  8.3 25.4 %broadcast_in_dim.7 = bf16[2048,32,128]{2,1,0:T(8,128)(2,1)S(1)} broadcast(bf16[2048,32]{1,0:T(8,128)(2,1)S(1)} %bitcast.70), dimensions={0,1} | broadcast | bytes 16908288 | tf_op jit(solution)/shard_map/broadcast_in_dim | solution.py:20
  33.7 14.5 %convert_reduce_fusion.1 = (f32[2048]{0:T(1024)S(1)}, f32[4096]{0:T(1024)S(1)}, bf16[2048,4096]{1,0:T(8,128)(2,1)}) fusion(bf16[256,8,32,128]{3,2,1,0:T(8,128)(2,1)S(1)} %bitcast.69, bf16[1,2048,4096]{2,1,0:T(8,128)(2,1)} %param.7), kind=kLoop, calls=%fused_computation.1 | loop fusion | flops 33548288 | bytes 50356224 | tf_op jit(solution)/shard_map/reduce_sum | solution.py:22
  48.2 5.0 fusion.5
  53.2 11.8 %fusion.15 = f32[64,2048]{1,0:T(8,128)} fusion(bf16[2048,4096]{1,0:T(8,128)(2,1)} %get-tuple-element.9, f32[64,1,4096]{2,1,0:T(1,128)S(1)} %fusion.5), kind=kOutput, calls=%fused_computation.24 | convolution fusion | flops 1073741824 | bytes 18350080 | tf_op jit(solution)/shard_map/dot_general | solution.py:39
  65.1 0.5 all-reduce.8.cloned.1.call-start
  65.6 39.2 %psum.43 = f32[2048]{0:T(1024)S(1)} all-reduce(f32[2048]{0:T(1024)S(1)} %get-tuple-element.5), channel_id=1, replica_groups=mesh['subset'=8,'tile'=16] {'tile'}, use_global_device_ids=true, to_apply=%region_2.3 | all-reduce | flops 2048 | bytes 16384 | tf_op jit(solution)/shard_map/psum | solution.py:32
  104.8 2.4 fusion.13
  107.1 100.0 %all-reduce.6.cloned.1.call-done = f32[64,2048]{1,0:T(8,128)} async-done(((f32[64,2048]{1,0:T(8,128)}), f32[64,2048]{1,0:T(8,128)}) %all-reduce.6.cloned.1.call-update) | async-done | bytes 524304 | tf_op jit(solution)/shard_map/psum | solution.py:42
  207.1 9.6 fusion.3
  216.7 1.2 collective-permute-start
  218.0 24.7 %collective-permute-done = f32[64,4096]{1,0:T(8,128)S(1)} collective-permute-done((f32[64,4096]{1,0:T(8,128)S(1)}, f32[64,4096]{1,0:T(8,128)S(1)}, u32[]{:S(2)}, u32[]{:S(2)}) %collective-permute-start) | collective-permute-done | bytes 1048608 | tf_op jit(solution)/shard_map/ppermute | solution.py:13
  242.6 11.7 %fusion.28 = f32[64,2048]{1,0:T(8,128)} fusion(bf16[2048,4096]{1,0:T(8,128)(2,1)} %get-tuple-element.9, f32[64,4096]{1,0:T(8,128)S(1)} %collective-permute-done), kind=kOutput, calls=%fused_computation.41 | convolution fusion | flops 1074003968 | bytes 18350080 | tf_op jit(solution)/shard_map/dot_general | solution.py:39
  254.7 2.4 fusion.11
  257.1 133.7 %all-reduce.8.cloned.1.call-done = f32[64,2048]{1,0:T(8,128)} async-done(((f32[64,2048]{1,0:T(8,128)}), f32[64,2048]{1,0:T(8,128)}) %all-reduce.8.cloned.1.call-update) | async-done | bytes 524304 | tf_op jit(solution)/shard_map/psum | solution.py:42
  390.8 9.2 fusion.2
  399.9 1.2 collective-permute-start.1
  401.1 24.7 %collective-permute-done.1 = f32[64,4096]{1,0:T(8,128)S(1)} collective-permute-done((f32[64,4096]{1,0:T(8,128)S(1)}, f32[64,4096]{1,0:T(8,128)S(1)}, u32[]{:S(2)}, u32[]{:S(2)}) %collective-permute-start.1) | collective-permute-done | bytes 1048608 | tf_op jit(solution)/shard_map/ppermute | solution.py:13
  425.8 11.7 %fusion.26 = f32[64,2048]{1,0:T(8,128)} fusion(bf16[2048,4096]{1,0:T(8,128)(2,1)} %get-tuple-element.9, f32[64,4096]{1,0:T(8,128)S(1)} %collective-permute-done.1), kind=kOutput, calls=%fused_computation.39 | convolution fusion | flops 1074003968 | bytes 18350080 | tf_op jit(solution)/shard_map/dot_general | solution.py:39
  437.7 2.4 fusion.9
  440.1 133.9 %all-reduce.10.cloned.1.call-done = f32[64,2048]{1,0:T(8,128)} async-done(((f32[64,2048]{1,0:T(8,128)}), f32[64,2048]{1,0:T(8,128)}) %all-reduce.10.cloned.1.call-update) | async-done | bytes 524304 | tf_op jit(solution)/shard_map/psum | solution.py:42
  573.9 9.2 fusion.1
  583.1 1.4 collective-permute-start.2
  584.5 24.7 %collective-permute-done.2 = f32[64,4096]{1,0:T(8,128)S(1)} collective-permute-done((f32[64,4096]{1,0:T(8,128)S(1)}, f32[64,4096]{1,0:T(8,128)S(1)}, u32[]{:S(2)}, u32[]{:S(2)}) %collective-permute-start.2) | collective-permute-done | bytes 1048608 | tf_op jit(solution)/shard_map/ppermute | solution.py:13
  609.2 11.7 %fusion.24 = f32[64,2048]{1,0:T(8,128)} fusion(bf16[2048,4096]{1,0:T(8,128)(2,1)} %get-tuple-element.9, f32[64,4096]{1,0:T(8,128)S(1)} %collective-permute-done.2), kind=kOutput, calls=%fused_computation.37 | convolution fusion | flops 1074003968 | bytes 18350080 | tf_op jit(solution)/shard_map/dot_general | solution.py:39
  621.1 2.4 fusion.7
  623.5 133.9 %all-reduce.12.cloned.1.call-done = f32[64,2048]{1,0:T(8,128)} async-done(((f32[64,2048]{1,0:T(8,128)}), f32[64,2048]{1,0:T(8,128)}) %all-reduce.12.cloned.1.call-update) | async-done | bytes 524304 | tf_op jit(solution)/shard_map/psum | solution.py:42
  757.3 9.2 fusion.4
  766.6 3.1 multiply_convert_fusion
  769.7 184.8 %all-reduce.14.cloned.1.call-done = bf16[8,64,4096]{2,1,0:T(8,128)(2,1)} async-done(((bf16[8,64,4096]{2,1,0:T(8,128)(2,1)}), bf16[8,64,4096]{2,1,0:T(8,128)(2,1)}) %all-reduce.14.cloned.1.call-update) | async-done | bytes 4194320 | tf_op jit(solution)/shard_map/psum | solution.py:51
  954.5 4.7 copy.46
  (19 shorter events, 1.0 us)
Async XLA Ops:
  6.5 98.2 %copy-start = (bf16[1,8,64,2048]{3,2,1,0:T(8,128)(2,1)S(1)}, bf16[1,8,64,2048]{3,2,1,0:T(8,128)(2,1)}, u32[]{:S(2)}) copy-start(bf16[1,8,64,2048]{3,2,1,0:T(8,128)(2,1)} %param.6) | copy-start | bytes 6291460
  6.5 200.6 %all-reduce.6.cloned.1.call-start = ((), (), s32[]{:S(2)}) async-start(), calls=%async_computation | async-start | bytes 1048576 | tf_op jit(solution)/shard_map/psum | solution.py:42
  33.7 14.5 %copy-start.1 = (bf16[8,64,4096]{2,1,0:T(8,128)(2,1)S(1)}, bf16[8,64,4096]{2,1,0:T(8,128)(2,1)}, u32[]{:S(2)}) copy-start(bf16[8,64,4096]{2,1,0:T(8,128)(2,1)} %param.5) | copy-start | bytes 12582916
  65.1 325.7 %all-reduce.8.cloned.1.call-start = ((), (), s32[]{:S(2)}) async-start(), calls=%async_computation.1 | async-start | bytes 1048576 | tf_op jit(solution)/shard_map/psum | solution.py:42
  216.7 25.9 %collective-permute-start = (f32[64,4096]{1,0:T(8,128)S(1)}, f32[64,4096]{1,0:T(8,128)S(1)}, u32[]{:S(2)}, u32[]{:S(2)}) collective-permute-start(f32[64,4096]{1,0:T(8,128)S(1)} %fusion.3), channel_id=1, source_target_pairs={{112,0},{0,16},{16,32},{32,48},{48,64},{64,80},{80,96},{96,112},{1... | collective-permute-start | bytes 3145736 | tf_op jit(solution)/shard_map/ppermute | solution.py:13
  254.4 319.6 %all-reduce.10.cloned.1.call-start = ((), (), s32[]{:S(2)}) async-start(), calls=%async_computation.2 | async-start | bytes 1048576 | tf_op jit(solution)/shard_map/psum | solution.py:42
  399.9 25.9 %collective-permute-start.1 = (f32[64,4096]{1,0:T(8,128)S(1)}, f32[64,4096]{1,0:T(8,128)S(1)}, u32[]{:S(2)}, u32[]{:S(2)}) collective-permute-start(f32[64,4096]{1,0:T(8,128)S(1)} %fusion.2), channel_id=1, source_target_pairs={{112,0},{0,16},{16,32},{32,48},{48,64},{64,80},{80,96},{96,112},{1... | collective-permute-start | bytes 3145736 | tf_op jit(solution)/shard_map/ppermute | solution.py:13
  437.5 319.8 %all-reduce.12.cloned.1.call-start = ((), (), s32[]{:S(2)}) async-start(), calls=%async_computation.3 | async-start | bytes 1048576 | tf_op jit(solution)/shard_map/psum | solution.py:42
  583.1 26.1 %collective-permute-start.2 = (f32[64,4096]{1,0:T(8,128)S(1)}, f32[64,4096]{1,0:T(8,128)S(1)}, u32[]{:S(2)}, u32[]{:S(2)}) collective-permute-start(f32[64,4096]{1,0:T(8,128)S(1)} %fusion.1), channel_id=1, source_target_pairs={{112,0},{0,16},{16,32},{32,48},{48,64},{64,80},{80,96},{96,112},{1... | collective-permute-start | bytes 3145736 | tf_op jit(solution)/shard_map/ppermute | solution.py:13
  620.9 333.6 %all-reduce.14.cloned.1.call-start = ((), (), s32[]{:S(2)}) async-start(), calls=%async_computation.4 | async-start | bytes 8388608 | tf_op jit(solution)/shard_map/psum | solution.py:51
Sparse Core Ops, SparseCore 0:
  65.2 141.8 all-reduce.5
  254.5 136.2 all-reduce.7
  437.7 136.2 all-reduce.9
  621.1 136.2 all-reduce.11
  769.8 184.6 all-reduce.13
where the time goes:
time: 975 us; the launch traced here: 966 us
  waiting for transfers between devices  760 us (78%)
  matrix products  98.5 us (10%)
  blocking collectives  39.2 us (4%)
  local copies, waits for them, and re-layouts  30.7 us (3%)
  other arithmetic  19.2 us (2%)
  between operations  13.4 us (1%)
    psum x4, waiting for transfers between devices, body(): projected = lax.psum(partial_value, 'tile')  501 us
    psum x1, waiting for transfers between devices, body(): gathered = lax.psum(contribution.astype(jnp.bfloat16), 'subset')  185 us
    ppermute x3, waiting for transfers between devices, passed_along(): return lax.ppermute(block, axis, route)  74 us
    dot_general x4, matrix products, body(): lax.dot_general(narrow, matrix, (((1,), (1,)), ((), ())), preferred_eleme...  47.1 us
    psum x1, blocking collectives, body(): ray_total = lax.psum(row_part, 'tile')  39.2 us
    dot_general x4, matrix products, body(): spread_back = jnp.dot(residue, matrix, preferred_element_type=jnp.float32)  37.1 us
    broadcast_in_dim x1, local copies, waits for them, and re-layouts, body(): jnp.repeat(jnp.repeat(pattern, BLOCK_SIDE, 0), BLOCK_SIDE, 1)  25.4 us
  transfers between devices with their start and end apart: 8, of which 8 were waited for; matrix products, arithmetic and copies ran while one was open for 1% of the time, Pallas kernels for 0%

commit v1 on v0

--- a/solution.py
+++ b/solution.py
@@ -39,7 +39,7 @@
         partial_value = lax.dot_general(
             narrow, matrix, (((1,), (1,)), ((), ())), preferred_element_type=jnp.float32
         )
-        projected = lax.psum(partial_value, "tile")
+        projected = jnp.sum(lax.all_gather(partial_value, "tile"), axis=0)
         residue = ((destination_rows - projected) / ray_total).astype(jnp.bfloat16)
         spread_back = jnp.dot(residue, matrix, preferred_element_type=jnp.float32)
         volume = volume + spread_back / column_sum[None, :]

time: 975 us -> 725 us (0.74)
  waiting for transfers between devices: 760 us -> 493 us
  other arithmetic: 19.2 us -> 38.2 us
    psum x4 -> x0, waiting for transfers between devices: 501 us -> none  [body(): projected = lax.psum(partial_value, 'tile')]
    all_gather x0 -> x4, waiting for transfers between devices: none -> 235 us  [body(): projected = jnp.sum(lax.all_gather(partial_value, 'tile'), axis=0)]
    reduce_sum x0 -> x4, other arithmetic: none -> 18.9 us  [body(): projected = jnp.sum(lax.all_gather(partial_value, 'tile'), axis=0)]
where the time goes in v1:
time: 725 us; the launch traced here: 717 us
  waiting for transfers between devices  493 us (68%)
  matrix products  98.7 us (14%)
  blocking collectives  39.3 us (5%)
  other arithmetic  38.2 us (5%)
  local copies, waits for them, and re-layouts  30.7 us (4%)
  between operations  13.5 us (2%)
    all_gather x4, waiting for transfers between devices, body(): projected = jnp.sum(lax.all_gather(partial_value, 'tile'), axis=0)  235 us
    psum x1, waiting for transfers between devices, body(): gathered = lax.psum(contribution.astype(jnp.bfloat16), 'subset')  181 us
    ppermute x3, waiting for transfers between devices, passed_along(): return lax.ppermute(block, axis, route)  76.6 us
    dot_general x4, matrix products, body(): lax.dot_general(narrow, matrix, (((1,), (1,)), ((), ())), preferred_eleme...  47.1 us
    psum x1, blocking collectives, body(): ray_total = lax.psum(row_part, 'tile')  39.3 us
    dot_general x4, matrix products, body(): spread_back = jnp.dot(residue, matrix, preferred_element_type=jnp.float32)  37.1 us
    broadcast_in_dim x1, local copies, waits for them, and re-layouts, body(): jnp.repeat(jnp.repeat(pattern, BLOCK_SIDE, 0), BLOCK_SIDE, 1)  25.4 us
    reduce_sum x4, other arithmetic, body(): projected = jnp.sum(lax.all_gather(partial_value, 'tile'), axis=0)  18.9 us
  transfers between devices with their start and end apart: 8, of which 8 were waited for; matrix products, arithmetic and copies ran while one was open for 1% of the time, Pallas kernels for 0%

profile of v1, /device:TPU:16, one launch (start us, length us, event | category | flops | bytes accessed | tf_op | source)
XLA Modules:
  0.0 716.6 jit_solution(11204942570828800561)
XLA Ops:
  6.5 0.8 convert_bitcast_fusion.1
  8.3 25.4 %broadcast_in_dim.7 = bf16[2048,32,128]{2,1,0:T(8,128)(2,1)S(1)} broadcast(bf16[2048,32]{1,0:T(8,128)(2,1)S(1)} %bitcast.78), dimensions={0,1} | broadcast | bytes 16908288 | tf_op jit(solution)/shard_map/broadcast_in_dim | solution.py:20
  33.7 14.5 %convert_reduce_fusion.1 = (f32[2048]{0:T(1024)S(1)}, f32[4096]{0:T(1024)S(1)}, bf16[2048,4096]{1,0:T(8,128)(2,1)}) fusion(bf16[256,8,32,128]{3,2,1,0:T(8,128)(2,1)S(1)} %bitcast.73, bf16[1,2048,4096]{2,1,0:T(8,128)(2,1)} %param.7), kind=kLoop, calls=%fused_computation.1 | loop fusion | flops 33548288 | bytes 50356224 | tf_op jit(solution)/shard_map/reduce_sum | solution.py:22
  48.2 5.0 fusion.5
  53.2 11.8 %fusion.15 = f32[64,2048]{1,0:T(8,128)} fusion(bf16[2048,4096]{1,0:T(8,128)(2,1)} %get-tuple-element.9, f32[64,1,4096]{2,1,0:T(1,128)S(1)} %fusion.5), kind=kOutput, calls=%fused_computation.24 | convolution fusion | flops 1073741824 | bytes 18350080 | tf_op jit(solution)/shard_map/dot_general | solution.py:39
  65.7 39.3 %psum.14 = f32[2048]{0:T(1024)S(1)} all-reduce(f32[2048]{0:T(1024)S(1)} %get-tuple-element.5), channel_id=1, replica_groups=mesh['subset'=8,'tile'=16] {'tile'}, use_global_device_ids=true, to_apply=%region_2.3 | all-reduce | flops 2048 | bytes 16384 | tf_op jit(solution)/shard_map/psum | solution.py:32
  105.0 2.4 fusion.13
  107.3 32.9 %all-gather.9.cloned.1.call-done = f32[1024,2048]{1,0:T(8,128)} async-done(((f32[64,2048]{1,0:T(8,128)}), f32[1024,2048]{1,0:T(8,128)}) %all-gather.9.cloned.1.call-update) | async-done | bytes 8388624 | tf_op jit(solution)/shard_map/all_gather | solution.py:42
  140.2 4.7 reduce_sum.54
  144.9 9.6 %fusion.3 = f32[64,4096]{1,0:T(8,128)S(1)} fusion(bf16[2048,4096]{1,0:T(8,128)(2,1)} %get-tuple-element.9, f32[64,1,4096]{2,1,0:T(1,128)S(1)} %fusion.5, f32[4096]{0:T(1024)S(1)} %get-tuple-element.6, f32[64,2048]{1,0:T(8,128)} %reduce_sum.54, f32[64,1,2048]{2,1,0:T(1,128)} %fusion.13, f32[2048]{0:T(1024)S(1)} %psum.14), kind=kOutput, calls=%fused_computation.11 | convolution fusion | flops 1074659328 | bytes 19947520 | tf_op jit(solution)/shard_map/dot_general | solution.py:44
  154.6 0.7 collective-permute-start
  155.3 25.5 %collective-permute-done = f32[64,4096]{1,0:T(8,128)S(1)} collective-permute-done((f32[64,4096]{1,0:T(8,128)S(1)}, f32[64,4096]{1,0:T(8,128)S(1)}, u32[]{:S(2)}, u32[]{:S(2)}) %collective-permute-start) | collective-permute-done | bytes 1048608 | tf_op jit(solution)/shard_map/ppermute | solution.py:13
  180.8 11.7 %fusion.28 = f32[64,2048]{1,0:T(8,128)} fusion(bf16[2048,4096]{1,0:T(8,128)(2,1)} %get-tuple-element.9, f32[64,4096]{1,0:T(8,128)S(1)} %collective-permute-done), kind=kOutput, calls=%fused_computation.41 | convolution fusion | flops 1074003968 | bytes 18350080 | tf_op jit(solution)/shard_map/dot_general | solution.py:39
  193.0 2.4 fusion.11
  195.3 67.3 %all-gather.11.cloned.1.call-done = f32[1024,2048]{1,0:T(8,128)} async-done(((f32[64,2048]{1,0:T(8,128)}), f32[1024,2048]{1,0:T(8,128)}) %all-gather.11.cloned.1.call-update) | async-done | bytes 8388624 | tf_op jit(solution)/shard_map/all_gather | solution.py:42
  262.7 4.7 reduce_sum.57
  267.4 9.2 %fusion.2 = f32[64,4096]{1,0:T(8,128)S(1)} fusion(f32[64,4096]{1,0:T(8,128)S(1)} %collective-permute-done, bf16[2048,4096]{1,0:T(8,128)(2,1)} %get-tuple-element.9, f32[4096]{0:T(1024)S(1)} %get-tuple-element.6, f32[64,2048]{1,0:T(8,128)} %reduce_sum.57, f32[64,1,2048]{2,1,0:T(1,128)} %fusion.11, f32[2048]{0:T(1024)S(1)} %psum.14), kind=kOutput, calls=%fused_computation.9 | convolution fusion | flops 1074659328 | bytes 19947520 | tf_op jit(solution)/shard_map/dot_general | solution.py:44
  277.3 25.5 %collective-permute-done.1 = f32[64,4096]{1,0:T(8,128)S(1)} collective-permute-done((f32[64,4096]{1,0:T(8,128)S(1)}, f32[64,4096]{1,0:T(8,128)S(1)}, u32[]{:S(2)}, u32[]{:S(2)}) %collective-permute-start.1) | collective-permute-done | bytes 1048608 | tf_op jit(solution)/shard_map/ppermute | solution.py:13
  302.8 11.7 %fusion.26 = f32[64,2048]{1,0:T(8,128)} fusion(bf16[2048,4096]{1,0:T(8,128)(2,1)} %get-tuple-element.9, f32[64,4096]{1,0:T(8,128)S(1)} %collective-permute-done.1), kind=kOutput, calls=%fused_computation.39 | convolution fusion | flops 1074003968 | bytes 18350080 | tf_op jit(solution)/shard_map/dot_general | solution.py:39
  315.0 2.4 fusion.9
  317.4 67.3 %all-gather.13.cloned.1.call-done = f32[1024,2048]{1,0:T(8,128)} async-done(((f32[64,2048]{1,0:T(8,128)}), f32[1024,2048]{1,0:T(8,128)}) %all-gather.13.cloned.1.call-update) | async-done | bytes 8388624 | tf_op jit(solution)/shard_map/all_gather | solution.py:42
  384.6 4.7 reduce_sum.58
  389.4 9.2 %fusion.1 = f32[64,4096]{1,0:T(8,128)S(1)} fusion(f32[64,4096]{1,0:T(8,128)S(1)} %collective-permute-done.1, bf16[2048,4096]{1,0:T(8,128)(2,1)} %get-tuple-element.9, f32[4096]{0:T(1024)S(1)} %get-tuple-element.6, f32[64,2048]{1,0:T(8,128)} %reduce_sum.58, f32[64,1,2048]{2,1,0:T(1,128)} %fusion.9, f32[2048]{0:T(1024)S(1)} %psum.14), kind=kOutput, calls=%fused_computation.7 | convolution fusion | flops 1074659328 | bytes 19947520 | tf_op jit(solution)/shard_map/dot_general | solution.py:44
  399.2 25.5 %collective-permute-done.2 = f32[64,4096]{1,0:T(8,128)S(1)} collective-permute-done((f32[64,4096]{1,0:T(8,128)S(1)}, f32[64,4096]{1,0:T(8,128)S(1)}, u32[]{:S(2)}, u32[]{:S(2)}) %collective-permute-start.2) | collective-permute-done | bytes 1048608 | tf_op jit(solution)/shard_map/ppermute | solution.py:13
  424.8 11.7 %fusion.24 = f32[64,2048]{1,0:T(8,128)} fusion(bf16[2048,4096]{1,0:T(8,128)(2,1)} %get-tuple-element.9, f32[64,4096]{1,0:T(8,128)S(1)} %collective-permute-done.2), kind=kOutput, calls=%fused_computation.37 | convolution fusion | flops 1074003968 | bytes 18350080 | tf_op jit(solution)/shard_map/dot_general | solution.py:39
  437.0 2.4 fusion.7
  439.4 67.2 %all-gather.15.cloned.1.call-done = f32[1024,2048]{1,0:T(8,128)} async-done(((f32[64,2048]{1,0:T(8,128)}), f32[1024,2048]{1,0:T(8,128)}) %all-gather.15.cloned.1.call-update) | async-done | bytes 8388624 | tf_op jit(solution)/shard_map/all_gather | solution.py:42
  506.6 4.7 reduce_sum.59
  511.3 9.2 %fusion.4 = bf16[64,4096]{1,0:T(8,128)(2,1)S(1)} fusion(f32[64,4096]{1,0:T(8,128)S(1)} %collective-permute-done.2, bf16[2048,4096]{1,0:T(8,128)(2,1)} %get-tuple-element.9, f32[4096]{0:T(1024)S(1)} %get-tuple-element.6, f32[64,2048]{1,0:T(8,128)} %reduce_sum.59, f32[64,1,2048]{2,1,0:T(1,128)} %fusion.7, f32[2048]{0:T(1024)S(1)} %psum.14), kind=kOutput, calls=%fused_computation.12 | convolution fusion | flops 1074921472 | bytes 19423232 | tf_op jit(solution)/shard_map/dot_general | solution.py:44
  520.6 3.1 multiply_convert_fusion
  523.7 181.4 %all-reduce.2.cloned.1.call-done = bf16[8,64,4096]{2,1,0:T(8,128)(2,1)} async-done(((bf16[8,64,4096]{2,1,0:T(8,128)(2,1)}), bf16[8,64,4096]{2,1,0:T(8,128)(2,1)}) %all-reduce.2.cloned.1.call-update) | async-done | bytes 4194320 | tf_op jit(solution)/shard_map/psum | solution.py:51
  705.1 4.7 copy.42
  (23 shorter events, 4.2 us)
Async XLA Ops:
  6.5 98.4 %copy-start = (bf16[1,8,64,2048]{3,2,1,0:T(8,128)(2,1)S(1)}, bf16[1,8,64,2048]{3,2,1,0:T(8,128)(2,1)}, u32[]{:S(2)}) copy-start(bf16[1,8,64,2048]{3,2,1,0:T(8,128)(2,1)} %param.6) | copy-start | bytes 6291460
  6.5 133.7 %all-gather.9.cloned.1.call-start = ((), (), s32[]{:S(2)}) async-start(), calls=%async_computation.1 | async-start | bytes 8912896 | tf_op jit(solution)/shard_map/all_gather | solution.py:42
  33.7 14.5 %copy-start.1 = (bf16[8,64,4096]{2,1,0:T(8,128)(2,1)S(1)}, bf16[8,64,4096]{2,1,0:T(8,128)(2,1)}, u32[]{:S(2)}) copy-start(bf16[8,64,4096]{2,1,0:T(8,128)(2,1)} %param.5) | copy-start | bytes 12582916
  65.1 197.6 %all-gather.11.cloned.1.call-start = ((), (), s32[]{:S(2)}) async-start(), calls=%async_computation.2 | async-start | bytes 8912896 | tf_op jit(solution)/shard_map/all_gather | solution.py:42
  154.6 26.3 %collective-permute-start = (f32[64,4096]{1,0:T(8,128)S(1)}, f32[64,4096]{1,0:T(8,128)S(1)}, u32[]{:S(2)}, u32[]{:S(2)}) collective-permute-start(f32[64,4096]{1,0:T(8,128)S(1)} %fusion.3), channel_id=1, source_target_pairs={{112,0},{0,16},{16,32},{32,48},{48,64},{64,80},{80,96},{96,112},{1... | collective-permute-start | bytes 3145736 | tf_op jit(solution)/shard_map/ppermute | solution.py:13
  192.6 192.0 %all-gather.13.cloned.1.call-start = ((), (), s32[]{:S(2)}) async-start(), calls=%async_computation.3 | async-start | bytes 8912896 | tf_op jit(solution)/shard_map/all_gather | solution.py:42
  276.5 26.3 %collective-permute-start.1 = (f32[64,4096]{1,0:T(8,128)S(1)}, f32[64,4096]{1,0:T(8,128)S(1)}, u32[]{:S(2)}, u32[]{:S(2)}) collective-permute-start(f32[64,4096]{1,0:T(8,128)S(1)} %fusion.2), channel_id=1, source_target_pairs={{112,0},{0,16},{16,32},{32,48},{48,64},{64,80},{80,96},{96,112},{1... | collective-permute-start | bytes 3145736 | tf_op jit(solution)/shard_map/ppermute | solution.py:13
  314.6 192.0 %all-gather.15.cloned.1.call-start = ((), (), s32[]{:S(2)}) async-start(), calls=%async_computation.4 | async-start | bytes 8912896 | tf_op jit(solution)/shard_map/all_gather | solution.py:42
  398.5 26.3 %collective-permute-start.2 = (f32[64,4096]{1,0:T(8,128)S(1)}, f32[64,4096]{1,0:T(8,128)S(1)}, u32[]{:S(2)}, u32[]{:S(2)}) collective-permute-start(f32[64,4096]{1,0:T(8,128)S(1)} %fusion.1), channel_id=1, source_target_pairs={{112,0},{0,16},{16,32},{32,48},{48,64},{64,80},{80,96},{96,112},{1... | collective-permute-start | bytes 3145736 | tf_op jit(solution)/shard_map/ppermute | solution.py:13
  436.6 268.5 %all-reduce.2.cloned.1.call-start = ((), (), s32[]{:S(2)}) async-start(), calls=%async_computation | async-start | bytes 8388608 | tf_op jit(solution)/shard_map/psum | solution.py:51
Sparse Core Ops, SparseCore 0:
  65.2 74.9 all-gather.8
  192.7 69.8 all-gather.10
  314.7 69.8 all-gather.12
  436.7 69.8 all-gather.14
  523.8 181.2 all-reduce.1
